TPU v7x, 32 devices: a whole 2x2x4 slice. The times are simulated.
32 devices in a mesh: prow: 8 (over y, x, core), pcol: 4 (over z).
Axes of the slice: x: 2, y: 2, z: 4, core: 2. Of those that a mesh axis runs over, the one named last changes fastest.
Arguments:
- inverse_trailing: bfloat16 [18432, 18432], P('prow', 'pcol'), may hold values from -6 to 6
- panel: bfloat16 [18432, 256], P('prow'), may hold values from -0.0625 to 0.0625
- supernode_inverse: float32 [256, 256], replicated, may hold values from -6 to 6
- block_live: int32 [72], replicated, may hold values from 0 to 1, as said below
Outputs:
- column_inverse: float32 [18432, 256], P('prow')
- diagonal_inverse: float32 [256, 256], replicated
Inputs may be any that keep to these rules, and one draw needn't show every extreme that they name: Each aligned group of 9 consecutive block rows (the rows of one index of prow) holds at least one block row with block_live 1.
All inputs are finite; a program needn't handle non-finite values.
Results may differ from a plain program's by a relative error of at most 0.0003.
Values may be sent and summed in bfloat16 or wider, within the bound.
No kernel may reach another device: no remote copies, remote signals or barrier semaphores. Data moves between devices by JAX's collectives and lax.ppermute only.
A program may use at most 128 MiB of HBM per device.

v0:
```python
import jax
import jax.numpy as jnp
from jax import lax
from jax.sharding import PartitionSpec as P


def from_root(block, axis, source):
    block = jnp.where(lax.axis_index(axis) == source, block, jnp.zeros_like(block))
    return lax.psum(block, axis)


def per_device(inverse_trailing, panel, supernode_inverse, block_live):
    rows_dev = panel.shape[0]
    width = panel.shape[1]
    col_count = inverse_trailing.shape[1]
    ratio = lax.axis_size("prow") // lax.axis_size("pcol")
    row_index = lax.axis_index("prow")
    col_index = lax.axis_index("pcol")
    live_all = jnp.repeat(block_live, width)
    col_live = lax.dynamic_slice_in_dim(live_all, col_index * col_count, col_count).astype(
        jnp.float32
    )
    row_live = lax.dynamic_slice_in_dim(live_all, row_index * rows_dev, rows_dev).astype(
        jnp.float32
    )
    partial_sum = jnp.zeros((rows_dev, width), jnp.float32)
    for half in range(ratio):
        received = from_root(panel, "prow", col_index * ratio + half)
        half_live = col_live[half * rows_dev : (half + 1) * rows_dev]
        masked_half = (received.astype(jnp.float32) * half_live[:, None]).astype(jnp.bfloat16)
        tile_cols = inverse_trailing[:, half * rows_dev : (half + 1) * rows_dev]
        partial_sum = partial_sum + jnp.dot(
            tile_cols, masked_half, preferred_element_type=jnp.float32
        )
    local_panel = panel.astype(jnp.float32) * row_live[:, None]
    contract_rows = (((0,), (0,)), ((), ()))
    total = lax.psum(partial_sum, "pcol")
    column_inverse = -total * row_live[:, None]
    term = lax.dot_general(
        local_panel, column_inverse, contract_rows, precision=lax.Precision.HIGHEST
    )
    diag_total = lax.psum(term, "prow")
    diagonal_inverse = supernode_inverse - diag_total
    return (column_inverse, diagonal_inverse)


def solution(mesh):
    in_specs = (P("prow", "pcol"), P("prow", None), P(), P())
    out_specs = (P("prow", None), P())
    return jax.shard_map(
        per_device, mesh=mesh, in_specs=in_specs, out_specs=out_specs, check_vma=False
    )
```

profile of v0, /device:TPU:0, one launch (start us, length us, event | category | flops | bytes accessed | tf_op | source)
XLA Modules:
  0.0 254.0 jit_solution(5009432006979550034)
XLA Ops:
  7.2 0.0 copy-start
  7.2 0.0 all-reduce.9.cloned.1.call-start
  7.2 2.8 %broadcast_select_fusion.1 = (bf16[2304,256]{1,0:T(8,128)(2,1)}, bf16[2304,256]{1,0:T(8,128)(2,1)}) fusion(bf16[2304,256]{1,0:T(8,128)(2,1)} %param.5, pred[]{:T(512)S(6)} %eq.6, pred[]{:T(512)S(6)} %eq.7), kind=kLoop, calls=%fused_computation.16 | loop fusion | flops 1179648 | bytes 3538946 | tf_op jit(solution)/shard_map/jit(_where)/select_n | solution.py:8
  10.1 0.0 all-reduce.9.cloned.1.call-update
  10.1 0.0 all-reduce.5.cloned.1.call-start
  10.2 0.0 copy-done
  10.2 0.1 broadcast_bitcast_fusion
  10.3 0.1 dynamic-slice_convert_fusion
  10.4 67.3 %all-reduce.9.cloned.1.call-done = (bf16[2304,256]{1,0:T(8,128)(2,1)}, bf16[2304,256]{1,0:T(8,128)(2,1)}) async-done(((bf16[2304,256]{1,0:T(8,128)(2,1)}, bf16[2304,256]{1,0:T(8,128)(2,1)}), (bf16[2304,256]{1,0:T(8,128)(2,1)}, bf16[2304,256]{1,0:T(8,128)(2,1)})) %all-reduce.9.cloned.1.call-update) | async-done | bytes 2359312 | tf_op jit(solution)/shard_map/psum | solution.py:9
  77.6 0.0 copy-start.3
  77.7 7.3 %fusion = f32[256,2304]{1,0:T(8,128)S(1)} fusion(bf16[2304,4608]{1,0:T(8,128)(2,1)} %param.4, bf16[2304,256]{1,0:T(8,128)(2,1)} %get-tuple-element.4, f32[2304]{0:T(1024)S(1)} %get-tuple-element.9), kind=kOutput, calls=%fused_computation | convolution fusion | flops 2719678464 | bytes 14164992 | tf_op jit(solution)/shard_map/dot_general | solution.py:32
  85.0 0.0 copy-done.3
  85.0 8.9 %fusion.7 = f32[2304,256]{0,1:T(8,128)} fusion(f32[256,2304]{1,0:T(8,128)S(1)} %fusion, bf16[2304,4608]{1,0:T(8,128)(2,1)} %param.4, bf16[2304,256]{1,0:T(8,128)(2,1)S(1)} %copy-done.3, f32[2304]{0:T(1024)S(1)} %get-tuple-element.8), kind=kOutput, calls=%fused_computation.5 | convolution fusion | flops 2720268288 | bytes 16524288 | tf_op jit(solution)/shard_map/dot_general | solution.py:32
  93.9 0.0 copy-start.1
  93.9 0.0 all-reduce.5.cloned.1.call-update
  93.9 0.0 all-reduce.7.cloned.1.call-start
  94.0 1.2 copy-done.1
  95.2 0.7 copy.6
  95.9 0.1 dynamic-slice_convert_fusion.1
  96.0 92.0 %all-reduce.5.cloned.1.call-done = f32[2304,256]{0,1:T(8,128)} async-done(((f32[2304,256]{0,1:T(8,128)}), f32[2304,256]{0,1:T(8,128)}) %all-reduce.5.cloned.1.call-update) | async-done | bytes 2359312 | tf_op jit(solution)/shard_map/psum | solution.py:37
  188.0 4.7 %fusion.10 = f32[256,256]{1,0:T(8,128)} fusion(bf16[2304,256]{0,1:T(8,128)(2,1)S(1)} %copy.6, f32[2304]{0:T(1024)S(1)} %dynamic-slice_convert_fusion.1, f32[2304,256]{0,1:T(8,128)} %all-reduce.5.cloned.1.call-done), kind=kOutput, calls=%fused_computation.6 | convolution fusion | flops 1814298624 | bytes 3810304 | tf_op jit(solution)/shard_map/dot_general | solution.py:39
  192.7 0.0 all-reduce.7.cloned.1.call-update
  192.7 1.8 negate_multiply_fusion
  194.6 0.0 copy-start.2
  194.6 2.0 copy.7
  196.5 49.3 %all-reduce.7.cloned.1.call-done = f32[256,256]{1,0:T(8,128)} async-done(((f32[256,256]{1,0:T(8,128)}), f32[256,256]{1,0:T(8,128)}) %all-reduce.7.cloned.1.call-update) | async-done | bytes 262160 | tf_op jit(solution)/shard_map/psum | solution.py:42
  245.8 0.0 copy-done.2
  245.8 1.7 sub.3
  (2 shorter events, 0.0 us)
Async XLA Ops:
  7.2 3.0 %copy-start = (s32[72]{0:T(128)S(1)}, s32[72]{0:T(128)}, u32[]{:S(2)}) copy-start(s32[72]{0:T(128)} %param.7) | copy-start | bytes 868
  7.2 70.5 %all-reduce.9.cloned.1.call-start = ((), (), s32[]{:S(2)}) async-start(), calls=%async_computation.2 | async-start | bytes 4718592 | tf_op jit(solution)/shard_map/psum | solution.py:9
  10.1 177.9 %all-reduce.5.cloned.1.call-start = ((), (), s32[]{:S(2)}) async-start(), calls=%async_computation | async-start | bytes 4718592 | tf_op jit(solution)/shard_map/psum | solution.py:37
  77.6 7.3 %copy-start.3 = (bf16[2304,256]{1,0:T(8,128)(2,1)S(1)}, bf16[2304,256]{1,0:T(8,128)(2,1)}, u32[]{:S(2)}) copy-start(bf16[2304,256]{1,0:T(8,128)(2,1)} %get-tuple-element.5) | copy-start | bytes 3538948
  93.9 1.3 copy-start.1
  93.9 151.9 %all-reduce.7.cloned.1.call-start = ((), (), s32[]{:S(2)}) async-start(), calls=%async_computation.1 | async-start | bytes 524288 | tf_op jit(solution)/shard_map/psum | solution.py:42
  194.6 51.2 %copy-start.2 = (f32[256,256]{1,0:T(8,128)S(1)}, f32[256,256]{1,0:T(8,128)}, u32[]{:S(2)}) copy-start(f32[256,256]{1,0:T(8,128)} %param.6) | copy-start | bytes 786436
Sparse Core Ops, SparseCore 0:
  11.9 65.7 all-reduce.8
  94.0 93.9 all-reduce.4
  192.9 52.9 all-reduce.6
where the time goes:
time: 254 us
  waiting for transfers between devices  209 us (82%)
  matrix products  20.9 us (8%)
  between operations  13.8 us (5%)
  other arithmetic  6.55 us (3%)
  local copies, waits for them, and re-layouts  4.01 us (2%)
    psum x1, waiting for transfers between devices, per_device(): total = lax.psum(partial_sum, 'pcol')  92 us
    psum x1, waiting for transfers between devices, from_root(): return lax.psum(block, axis)  67.3 us
    psum x1, waiting for transfers between devices, per_device(): diag_total = lax.psum(term, 'prow')  49.3 us
    dot_general x2, matrix products, per_device(): jnp.dot(tile_cols, masked_half, preferred_element_type=jnp.float32)  16.2 us
  transfers between devices with their start and end apart: 3, of which 3 were waited for; matrix products, arithmetic and copies ran while one was open for 2% of the time, Pallas kernels for 0%

commit v1 on v0

--- a/solution.py
+++ b/solution.py
@@ -34,7 +34,16 @@
         )
     local_panel = panel.astype(jnp.float32) * row_live[:, None]
     contract_rows = (((0,), (0,)), ((), ()))
-    total = lax.psum(partial_sum, "pcol")
+
+    def turn_lots_all(xs):
+        extent = lax.axis_size("pcol")
+        block_out = xs
+        for dd in [[(ii, ii ^ h) for ii in range(extent)] for h in (1, 2, 4, 8, 16) if h < extent]:
+            mixed_arr = lax.ppermute(block_out, "pcol", dd)
+            block_out = block_out + mixed_arr
+        return block_out
+
+    total = turn_lots_all(partial_sum)
     column_inverse = -total * row_live[:, None]
     term = lax.dot_general(
         local_panel, column_inverse, contract_rows, precision=lax.Precision.HIGHEST

time: 254 us -> 316 us (1.24)
  waiting for transfers between devices: 209 us -> 269 us
  starting transfers between devices: 0.12 us -> 4.1 us
  matrix products: 20.9 us -> 17.2 us
    ppermute x0 -> x2, waiting for transfers between devices: none -> 148 us  [turn_lots_all(): mixed_arr = lax.ppermute(block_out, 'pcol', dd)]
    psum x1 -> x0, waiting for transfers between devices: 92 us -> none  [per_device(): total = lax.psum(partial_sum, 'pcol')]
    ppermute x0 -> x2, starting transfers between devices: none -> 4.02 us  [turn_lots_all(): mixed_arr = lax.ppermute(block_out, 'pcol', dd)]
    psum x1, waiting for transfers between devices: 49.3 us -> 52.9 us  [per_device(): diag_total = lax.psum(term, 'prow')]
  transfers between devices with their start and end apart: 3 -> 4, of which waited for: 3 -> 4; matrix products, arithmetic and copies ran while one was open for 2% -> 1% of each run, Pallas kernels for 0% -> 0%
where the time goes in v1:
time: 316 us
  waiting for transfers between devices  269 us (85%)
  matrix products  17.2 us (5%)
  between operations  14.2 us (4%)
  other arithmetic  8.3 us (3%)
  starting transfers between devices  4.1 us (1%)
  local copies, waits for them, and re-layouts  3.64 us (1%)
    ppermute x2, waiting for transfers between devices, turn_lots_all(): mixed_arr = lax.ppermute(block_out, 'pcol', dd)  148 us
    psum x1, waiting for transfers between devices, from_root(): return lax.psum(block, axis)  67.2 us
    psum x1, waiting for transfers between devices, per_device(): diag_total = lax.psum(term, 'prow')  52.9 us
    dot_general x2, matrix products, per_device(): jnp.dot(tile_cols, masked_half, preferred_element_type=jnp.float32)  14.3 us
  transfers between devices with their start and end apart: 4, of which 4 were waited for; matrix products, arithmetic and copies ran while one was open for 1% of the time, Pallas kernels for 0%

profile of v1, /device:TPU:0, one launch (start us, length us, event | category | flops | bytes accessed | tf_op | source)
XLA Modules:
  0.0 316.1 jit_solution(18272764766984340585)
XLA Ops:
  7.2 0.0 copy-start
  7.2 0.0 all-reduce.6.cloned.1.call-start
  7.2 2.9 broadcast_select_fusion.1
  10.1 0.0 all-reduce.6.cloned.1.call-update
  10.1 0.0 all-reduce.4.cloned.1.call-start
  10.2 0.0 copy-done
  10.2 0.1 broadcast_bitcast_fusion
  10.3 0.0 copy-start.5
  10.3 0.1 dynamic-slice_convert_fusion
  10.4 67.2 %all-reduce.6.cloned.1.call-done = (bf16[2304,256]{1,0:T(8,128)(2,1)}, bf16[2304,256]{1,0:T(8,128)(2,1)}) async-done(((bf16[2304,256]{1,0:T(8,128)(2,1)}, bf16[2304,256]{1,0:T(8,128)(2,1)}), (bf16[2304,256]{1,0:T(8,128)(2,1)}, bf16[2304,256]{1,0:T(8,128)(2,1)})) %all-reduce.6.cloned.1.call-update) | async-done | bytes 2359312 | tf_op jit(solution)/shard_map/psum | solution.py:9
  77.6 0.0 copy-start.6
  77.7 7.3 %fusion = f32[256,2304]{1,0:T(8,128)S(1)} fusion(bf16[2304,4608]{1,0:T(8,128)(2,1)} %param.4, bf16[2304,256]{1,0:T(8,128)(2,1)} %get-tuple-element.4, f32[2304]{0:T(1024)S(1)} %get-tuple-element.9), kind=kOutput, calls=%fused_computation | convolution fusion | flops 2719678464 | bytes 14164992 | tf_op jit(solution)/shard_map/dot_general | solution.py:32
  85.0 0.0 copy-done.5
  85.0 0.0 copy-done.6
  85.0 7.0 %fusion.7 = f32[2304,256]{0,1:T(8,128)S(1)} fusion(f32[256,2304]{1,0:T(8,128)S(1)} %fusion, bf16[2304,4608]{1,0:T(8,128)(2,1)} %param.4, bf16[2304,256]{1,0:T(8,128)(2,1)S(1)} %copy-done.6, f32[2304]{0:T(1024)S(1)} %get-tuple-element.8), kind=kOutput, calls=%fused_computation.5 | convolution fusion | flops 2720268288 | bytes 16524288 | tf_op jit(solution)/shard_map/dot_general | solution.py:32
  92.0 0.0 copy-start.2
  92.0 1.5 collective-permute-start
  93.6 50.5 %collective-permute-done = f32[2304,256]{0,1:T(8,128)S(1)} collective-permute-done((f32[2304,256]{0,1:T(8,128)S(1)}, f32[2304,256]{0,1:T(8,128)S(1)}, u32[]{:S(2)}, u32[]{:S(2)}) %collective-permute-start) | collective-permute-done | bytes 2359328 | tf_op jit(solution)/shard_map/ppermute | solution.py:42
  144.1 0.2 add.31
  144.3 0.0 copy-start.1
  144.3 2.5 collective-permute-start.1
  146.8 0.0 copy-done.2
  146.8 1.5 copy.6
  148.3 0.8 dynamic-slice_convert_fusion.1
  149.1 0.0 copy-done.1
  149.1 0.0 copy-start.3
  149.1 97.9 %collective-permute-done.1 = f32[2304,256]{0,1:T(8,128)} collective-permute-done((f32[2304,256]{0,1:T(8,128)S(1)}, f32[2304,256]{0,1:T(8,128)}, u32[]{:S(2)}, u32[]{:S(2)}) %collective-permute-start.1) | collective-permute-done | bytes 2359328 | tf_op jit(solution)/shard_map/ppermute | solution.py:42
  247.1 2.6 negate_multiply_fusion
  249.7 0.0 copy-done.3
  249.7 2.9 fusion.10
  252.6 0.0 all-reduce.4.cloned.1.call-update
  252.6 0.0 copy-start.4
  252.7 2.0 copy.7
  254.6 52.9 %all-reduce.4.cloned.1.call-done = f32[256,256]{1,0:T(8,128)} async-done(((f32[256,256]{1,0:T(8,128)}), f32[256,256]{1,0:T(8,128)}) %all-reduce.4.cloned.1.call-update) | async-done | bytes 262160 | tf_op jit(solution)/shard_map/psum | solution.py:51
  307.5 0.0 copy-done.4
  307.5 1.7 sub.3
  (2 shorter events, 0.0 us)
Async XLA Ops:
  7.2 3.0 copy-start
  7.2 70.5 %all-reduce.6.cloned.1.call-start = ((), (), s32[]{:S(2)}) async-start(), calls=%async_computation.1 | async-start | bytes 4718592 | tf_op jit(solution)/shard_map/psum | solution.py:9
  10.1 297.4 %all-reduce.4.cloned.1.call-start = ((), (), s32[]{:S(2)}) async-start(), calls=%async_computation | async-start | bytes 524288 | tf_op jit(solution)/shard_map/psum | solution.py:51
  10.3 74.7 %copy-start.5 = (s32[9,2,8,128]{3,1,2,0:T(2,128)}, s32[9,2,8,128]{3,1,2,0:T(2,128)S(1)}, u32[]{:S(2)}) copy-start(s32[9,2,8,128]{3,1,2,0:T(2,128)S(1)} %copy.8) | copy-start | bytes 221188
  77.6 7.3 %copy-start.6 = (bf16[2304,256]{1,0:T(8,128)(2,1)S(1)}, bf16[2304,256]{1,0:T(8,128)(2,1)}, u32[]{:S(2)}) copy-start(bf16[2304,256]{1,0:T(8,128)(2,1)} %get-tuple-element.5) | copy-start | bytes 3538948
  92.0 54.8 %copy-start.2 = (bf16[2304,256]{1,0:T(8,128)(2,1)S(1)}, bf16[2304,256]{1,0:T(8,128)(2,1)}, u32[]{:S(2)}) copy-start(bf16[2304,256]{1,0:T(8,128)(2,1)} %param.5) | copy-start | bytes 3538948
  92.0 52.0 %collective-permute-start = (f32[2304,256]{0,1:T(8,128)S(1)}, f32[2304,256]{0,1:T(8,128)S(1)}, u32[]{:S(2)}, u32[]{:S(2)}) collective-permute-start(f32[2304,256]{0,1:T(8,128)S(1)} %fusion.7), channel_id=1, source_target_pairs={{0,1},{1,0},{2,3},{3,2},{4,5},{5,4},{6,7},{7,6},{8,9},{9,8},{10,11... | collective-permute-start | bytes 7077896 | tf_op jit(solution)/shard_map/ppermute | solution.py:42
  144.3 4.8 %copy-start.1 = (f32[2304,256]{0,1:T(8,128)}, f32[2304,256]{0,1:T(8,128)S(1)}, u32[]{:S(2)}) copy-start(f32[2304,256]{0,1:T(8,128)S(1)} %add.31) | copy-start | bytes 7077892
  144.3 102.8 %collective-permute-start.1 = (f32[2304,256]{0,1:T(8,128)S(1)}, f32[2304,256]{0,1:T(8,128)}, u32[]{:S(2)}, u32[]{:S(2)}) collective-permute-start(f32[2304,256]{0,1:T(8,128)S(1)} %add.31), channel_id=1, source_target_pairs={{0,2},{1,3},{2,0},{3,1},{4,6},{5,7},{6,4},{7,5},{8,10},{9,11},{10,... | collective-permute-start | bytes 7077896 | tf_op jit(solution)/shard_map/ppermute | solution.py:42
  149.1 100.6 %copy-start.3 = (bf16[2304,256]{0,1:T(8,128)(2,1)S(1)}, bf16[2304,256]{0,1:T(8,128)(2,1)}, u32[]{:S(2)}) copy-start(bf16[2304,256]{0,1:T(8,128)(2,1)} %copy.6) | copy-start | bytes 3538948
  252.6 54.9 %copy-start.4 = (f32[256,256]{1,0:T(8,128)S(1)}, f32[256,256]{1,0:T(8,128)}, u32[]{:S(2)}) copy-start(f32[256,256]{1,0:T(8,128)} %param.6) | copy-start | bytes 786436
Sparse Core Ops, SparseCore 0:
  11.9 65.7 all-reduce.5
  252.8 54.7 all-reduce.3
